TPU v7x, 256 devices: a whole 4x4x8 slice. The times are simulated.
256 devices in a mesh: lon: 8 (over z), lat: 8 (over x, y_hi), dp: 4 (over y_lo, core).
Axes of the slice: x: 4, y: 4 (y_hi: 2, y_lo: 2; y = y_hi * 2 + y_lo), z: 8, core: 2. Of those that a mesh axis runs over, the one named last changes fastest.
Arguments:
- fields: bfloat16 [4, 256, 64, 1024], P('dp', None, 'lat', 'lon'), may hold values from -6 to 6
- weight_one: bfloat16 [9, 256, 256], replicated, may hold values from -0.125 to 0.125
- weight_two: bfloat16 [9, 256, 256], replicated, may hold values from -0.125 to 0.125
- edge_flips: int32 [7, 8], replicated, may hold values from 0 to 1, as said below
- cotangent: bfloat16 [4, 256, 64, 1024], P('dp', None, 'lat', 'lon'), may hold values from -6 to 6
Outputs:
- output: bfloat16 [4, 256, 64, 1024], P('dp', None, 'lat', 'lon')
- grad_fields: bfloat16 [4, 256, 64, 1024], P('dp', None, 'lat', 'lon')
- grad_one: float32 [9, 256, 256], replicated
- grad_two: float32 [9, 256, 256], replicated
Inputs may be any that keep to these rules, and one draw needn't show every extreme that they name: `edge_flips`: 0 on every edge inside a face; only row 8 // 2 - 1, the boundary between the band's two face rows, may hold 1, where the two faces meeting at that longitude tile store longitude in opposite orders.
All inputs are finite; a program needn't handle non-finite values.
Results may differ from a plain program's by a relative error of at most 0.0034.
Values may be sent and summed in bfloat16 or wider, within the bound.
No kernel may reach another device: no remote copies, remote signals or barrier semaphores. Data moves between devices by JAX's collectives and lax.ppermute only.
A program may use at most 128 MiB of HBM per device.

v0:
```python
import jax
import jax.numpy as jnp
from jax import lax
from jax.sharding import PartitionSpec as P


def with_halo(cells, sides, width, closed):
    for axis, dim in sides:
        count = lax.axis_size(axis)
        ends = count if closed else count - 1
        head = lax.slice_in_dim(cells, 0, width, axis=dim)
        tail = lax.slice_in_dim(cells, cells.shape[dim] - width, cells.shape[dim], axis=dim)
        cells = jnp.concatenate(
            [
                lax.ppermute(tail, axis, [(i, (i + 1) % count) for i in range(ends)]),
                cells,
                lax.ppermute(head, axis, [((i + 1) % count, i) for i in range(ends)]),
            ],
            axis=dim,
        )
    return cells


def oriented(line_cells, reverse_flag):
    return jnp.where(reverse_flag == 1, jnp.flip(line_cells, -1), line_cells)


def edge_flags(edge_flips):
    lat_index = lax.axis_index("lat")
    lon_index = lax.axis_index("lon")
    lat_count = lax.axis_size("lat")
    upper_flip = lax.dynamic_slice(edge_flips, (jnp.maximum(lat_index - 1, 0), lon_index), (1, 1))[
        0, 0
    ]
    lower_flip = lax.dynamic_slice(
        edge_flips, (jnp.minimum(lat_index, lat_count - 2), lon_index), (1, 1)
    )[0, 0]
    return (upper_flip, lower_flip, lat_index > 0, lat_index < lat_count - 1)


def padded(source, edge_info):
    upper_flip, lower_flip, has_upper, has_lower = edge_info
    extended = with_halo(source, (("lon", 3), ("lat", 2)), 1, True)
    top_rim = jnp.where(has_upper, extended[:, :, 0, :], jnp.zeros_like(extended[:, :, 0, :]))
    bottom = jnp.where(has_lower, extended[:, :, -1, :], jnp.zeros_like(extended[:, :, -1, :]))
    top_rim = oriented(top_rim, upper_flip)
    bottom = oriented(bottom, lower_flip)
    return jnp.concatenate(
        [top_rim[:, :, None, :], extended[:, :, 1:-1, :], bottom[:, :, None, :]], 2
    )


def patches_of(padded_in, tile_rows, tile_cols):
    return jnp.stack(
        [
            padded_in[:, :, tap_row : tap_row + tile_rows, tap_col : tap_col + tile_cols]
            for tap_row in range(3)
            for tap_col in range(3)
        ],
        1,
    )


def convolve(patches, weight):
    return jnp.einsum("toc,btchw->bohw", weight, patches, preferred_element_type=jnp.float32)


def transposed(grad_tile, weight, tile_rows, tile_cols):
    batch, chans = (grad_tile.shape[0], weight.shape[2])
    padded_grad = jnp.zeros((batch, chans, tile_rows + 2, tile_cols + 2), jnp.float32)
    for tap_row in range(3):
        for tap_col in range(3):
            tap_term = jnp.einsum(
                "oc,bohw->bchw",
                weight[3 * tap_row + tap_col],
                grad_tile,
                preferred_element_type=jnp.float32,
            )
            padded_grad = padded_grad.at[
                :, :, tap_row : tap_row + tile_rows, tap_col : tap_col + tile_cols
            ].add(tap_term)
    return padded_grad


def returned(padded_grad, edge_info):
    upper_flip, lower_flip, has_upper, has_lower = edge_info
    top_rim = oriented(padded_grad[:, :, 0, :], upper_flip)
    bottom = oriented(padded_grad[:, :, -1, :], lower_flip)
    rim_rows = jnp.stack([top_rim, bottom], 2)
    received = with_halo(rim_rows, (("lat", 2),), 1, False)
    interior = padded_grad[:, :, 1:-1, :]
    interior = interior.at[:, :, 0, :].add(received[:, :, 0, :])
    interior = interior.at[:, :, -1, :].add(received[:, :, -1, :])
    side_cols = jnp.stack([interior[..., 0], interior[..., -1]], -1)
    beside = with_halo(side_cols, (("lon", 3),), 1, True)
    result = interior[..., 1:-1]
    result = result.at[..., 0].add(beside[..., 0])
    result = result.at[..., -1].add(beside[..., -1])
    return result


def per_device(fields, weight_one, weight_two, edge_flips, cotangent):
    tile_rows, tile_cols = (fields.shape[2], fields.shape[3])
    edge_info = edge_flags(edge_flips)
    patch_in = patches_of(padded(fields, edge_info), tile_rows, tile_cols)
    hidden = convolve(patch_in, weight_one)
    activation = jax.nn.silu(hidden).astype(jnp.bfloat16)
    patch_act = patches_of(padded(activation, edge_info), tile_rows, tile_cols)
    output = (fields.astype(jnp.float32) + convolve(patch_act, weight_two)).astype(jnp.bfloat16)
    local_two = jnp.einsum(
        "bohw,btchw->toc", cotangent, patch_act, preferred_element_type=jnp.float32
    )
    back_act = returned(transposed(cotangent, weight_two, tile_rows, tile_cols), edge_info)
    sigmoid_h = jax.nn.sigmoid(hidden)
    back_hidden = (back_act * sigmoid_h * (1.0 + hidden * (1.0 - sigmoid_h))).astype(jnp.bfloat16)
    local_one = jnp.einsum(
        "bohw,btchw->toc", back_hidden, patch_in, preferred_element_type=jnp.float32
    )
    grad_one, grad_two = lax.psum((local_one, local_two), ("lon", "lat", "dp"))
    back_fields = returned(transposed(back_hidden, weight_one, tile_rows, tile_cols), edge_info)
    grad_fields = (cotangent.astype(jnp.float32) + back_fields).astype(jnp.bfloat16)
    return (output, grad_fields, grad_one, grad_two)


def solution(mesh):
    in_specs = (P("dp", None, "lat", "lon"), P(), P(), P(), P("dp", None, "lat", "lon"))
    out_specs = (P("dp", None, "lat", "lon"), P("dp", None, "lat", "lon"), P(), P())
    return jax.shard_map(
        per_device, mesh=mesh, in_specs=in_specs, out_specs=out_specs, check_vma=False
    )
```

profile of v0, /device:TPU:97, one launch (start us, length us, event | category | flops | bytes accessed | tf_op | source)
XLA Modules:
  0.0 453.6 jit_solution(17974031605681476931)
XLA Ops:
  8.6 2.9 collective-permute-start
  15.6 2.5 fusion.20
  18.1 4.0 scatter-add.89
  22.1 3.2 add_select_fusion.1
  25.3 4.0 scatter-add.90
  31.9 2.7 scatter-add.94
  35.9 2.7 scatter-add.95
  41.1 2.7 scatter-add.99
  45.1 2.7 scatter-add.100
  51.2 5.2 %collective-permute-start.3 = (bf16[1,256,1,130]{1,3,2,0:T(8,128)(2,1)S(1)}, bf16[1,256,1,130]{1,3,2,0:T(8,128)(2,1)S(1)}, u32[]{:S(2)}, u32[]{:S(2)}) collective-permute-start(bf16[1,256,1,130]{1,3,2,0:T(8,128)(2,1)S(1)} %get-tuple-element.342), channel_id=1, source_target_pairs={{4,0},{8,4},{12,8},{16,12},{20,16},{24,20},{28,24},{0,28},{5,1},{9... | collective-permute-start | bytes 199688 | tf_op jit(solution)/shard_map/ppermute | solution.py:17
  57.8 5.5 %collective-permute-start.8 = (f32[1,256,1,130]{1,3,2,0:T(8,128)S(1)}, f32[1,256,1,130]{1,3,2,0:T(8,128)S(1)}, u32[]{:S(2)}, u32[]{:S(2)}) collective-permute-start(f32[1,256,1,130]{1,3,2,0:T(8,128)S(1)} %get-tuple-element.327), channel_id=1, source_target_pairs={{0,4},{4,8},{8,12},{12,16},{16,20},{20,24},{24,28},{1,5},{5,9},{9,... | collective-permute-start | bytes 399368 | tf_op jit(solution)/shard_map/ppermute | solution.py:15
  64.7 6.4 %collective-permute-done.2 = bf16[1,256,1,130]{1,3,2,0:T(8,128)(2,1)S(1)} collective-permute-done((bf16[1,256,1,130]{1,3,2,0:T(8,128)(2,1)S(1)}, bf16[1,256,1,130]{1,3,2,0:T(8,128)(2,1)S(1)}, u32[]{:S(2)}, u32[]{:S(2)}) %collective-permute-start.2) | collective-permute-done | bytes 66592 | tf_op jit(solution)/shard_map/ppermute | solution.py:15
  73.6 2.7 collective-permute-start.10
  85.7 4.4 multiply_convert_fusion
  90.1 2.9 fusion.8
  93.3 2.6 fusion.29
  97.6 7.2 %scatter-add.110 = f32[1,256,10,130]{1,3,2,0:T(8,128)S(1)} dynamic-update-slice(f32[1,256,10,130]{1,3,2,0:T(8,128)S(1)} %scatter-add.109, f32[1,256,8,128]{1,3,2,0:T(8,128)} %fusion.29, s32[]{:T(128)} %constant.657.clone.1, s32[]{:T(128)} %constant.657.clone.1, s32[]{:T(128)} %bitcast.51, s32[]{:T(128)} %bitcast.52) | dynamic-update-slice | bytes 2097156 | tf_op jit(solution)/shard_map/scatter-add | solution.py:81
  104.8 4.1 add_select_fusion
  108.9 7.2 %scatter-add.111 = f32[1,256,10,130]{1,3,2,0:T(8,128)S(1)} dynamic-update-slice(f32[1,256,10,130]{1,3,2,0:T(8,128)S(1)} %scatter-add.110, f32[1,256,8,128]{1,3,2,0:T(8,128)} %add_select_fusion, s32[]{:T(128)} %constant.657.clone.1, s32[]{:T(128)} %constant.657.clone.1, s32[]{:T(128)} %bitcast.57, s32[]{:T(128)} %bitcast.58) | dynamic-update-slice | bytes 2097156 | tf_op jit(solution)/shard_map/scatter-add | solution.py:81
  119.5 5.9 %scatter-add.115 = f32[1,256,10,130]{1,3,2,0:T(8,128)S(1)} dynamic-update-slice(f32[1,256,10,130]{1,3,2,0:T(8,128)S(1)} %fusion.31, f32[1,256,8,128]{1,3,2,0:T(8,128)} %fusion.32, s32[]{:T(128)} %constant.657.clone.1, s32[]{:T(128)} %constant.657.clone.1, s32[]{:T(128)} %constant.670.clone.1, s32[]{:T(128)} %constant.670.clone.1) | dynamic-update-slice | bytes 2097156 | tf_op jit(solution)/shard_map/scatter-add | solution.py:81
  127.6 5.9 %scatter-add.116 = f32[1,256,10,130]{1,3,2,0:T(8,128)S(1)} dynamic-update-slice(f32[1,256,10,130]{1,3,2,0:T(8,128)S(1)} %scatter-add.115, f32[1,256,8,128]{1,3,2,0:T(8,128)} %fusion.33, s32[]{:T(128)} %constant.657.clone.1, s32[]{:T(128)} %constant.657.clone.1, s32[]{:T(128)} %constant.670.clone.1, s32[]{:T(128)} %constant.667.clone.1) | dynamic-update-slice | bytes 2097156 | tf_op jit(solution)/shard_map/scatter-add | solution.py:81
  136.8 5.9 %scatter-add.120 = f32[1,256,10,130]{1,3,2,0:T(8,128)S(1)} dynamic-update-slice(f32[1,256,10,130]{1,3,2,0:T(8,128)S(1)} %fusion.35, f32[1,256,8,128]{1,3,2,0:T(8,128)} %fusion.36, s32[]{:T(128)} %constant.657.clone.1, s32[]{:T(128)} %constant.657.clone.1, s32[]{:T(128)} %constant.667.clone.1, s32[]{:T(128)} %constant.670.clone.1) | dynamic-update-slice | bytes 2097156 | tf_op jit(solution)/shard_map/scatter-add | solution.py:81
  145.6 5.9 %scatter-add.121 = f32[1,256,10,130]{1,3,2,0:T(8,128)S(1)} dynamic-update-slice(f32[1,256,10,130]{1,3,2,0:T(8,128)S(1)} %scatter-add.120, f32[1,256,8,128]{1,3,2,0:T(8,128)} %fusion.37, s32[]{:T(128)} %constant.657.clone.1, s32[]{:T(128)} %constant.657.clone.1, s32[]{:T(128)} %constant.667.clone.1, s32[]{:T(128)} %constant.667.clone.1) | dynamic-update-slice | bytes 2097156 | tf_op jit(solution)/shard_map/scatter-add | solution.py:81
  151.5 3.0 collective-permute-start.6
  155.7 2.6 collective-permute-done.6
  162.9 2.9 fusion.11
  166.5 3.0 collective-permute-start.12
  171.4 6.0 %collective-permute-done.13 = f32[1,256,1,130]{1,3,2,0:T(8,128)S(1)} collective-permute-done((f32[1,256,1,130]{1,3,2,0:T(8,128)S(1)}, f32[1,256,1,130]{1,3,2,0:T(8,128)S(1)}, u32[]{:S(2)}, u32[]{:S(2)}) %collective-permute-start.13) | collective-permute-done | bytes 133152 | tf_op jit(solution)/shard_map/ppermute | solution.py:17
  180.2 3.8 fusion.41
  185.4 3.6 collective-permute-done.15
  190.3 251.3 %all-reduce.5.cloned.1.call-done = (f32[9,256,256]{1,2,0:T(8,128)}, f32[9,256,256]{1,2,0:T(8,128)}) async-done(((f32[9,256,256]{1,2,0:T(8,128)}, f32[9,256,256]{1,2,0:T(8,128)}), (f32[9,256,256]{1,2,0:T(8,128)}, f32[9,256,256]{1,2,0:T(8,128)})) %all-reduce.5.cloned.1.call-update) | async-done | bytes 4718608 | tf_op jit(solution)/shard_map/psum | solution.py:119
  441.6 3.2 copy.38
  (136 shorter events, 58.9 us)
Async XLA Ops:
  7.2 7.0 %copy-start = (bf16[1,256,8,128]{3,2,1,0:T(8,128)(2,1)S(1)}, bf16[1,256,8,128]{3,2,1,0:T(8,128)(2,1)}, u32[]{:S(2)}) copy-start(bf16[1,256,8,128]{3,2,1,0:T(8,128)(2,1)} %param.61) | copy-start | bytes 1572868
  7.2 434.4 %all-reduce.5.cloned.1.call-start = ((), (), s32[]{:S(2)}) async-start(), calls=%async_computation | async-start | bytes 9437184 | tf_op jit(solution)/shard_map/psum | solution.py:119
  8.6 42.5 %collective-permute-start = (bf16[1,256,8,1]{1,3,2,0:T(2,128)(2,1)S(1)}, bf16[1,256,8,1]{1,3,2,0:T(2,128)(2,1)S(1)}, u32[]{:S(2)}, u32[]{:S(2)}) collective-permute-start(bf16[1,256,8,1]{1,3,2,0:T(2,128)(2,1)S(1)} %get-tuple-element.346), channel_id=1, source_target_pairs={{0,32},{32,64},{64,96},{96,128},{128,160},{160,192},{192,224},{224... | collective-permute-start | bytes 12296 | tf_op jit(solution)/shard_map/ppermute | solution.py:15
  11.5 39.6 %collective-permute-start.1 = (bf16[1,256,8,1]{1,3,2,0:T(2,128)(2,1)S(1)}, bf16[1,256,8,1]{1,3,2,0:T(2,128)(2,1)S(1)}, u32[]{:S(2)}, u32[]{:S(2)}) collective-permute-start(bf16[1,256,8,1]{1,3,2,0:T(2,128)(2,1)S(1)} %get-tuple-element.347), channel_id=1, source_target_pairs={{32,0},{64,32},{96,64},{128,96},{160,128},{192,160},{224,192},{0,2... | collective-permute-start | bytes 12296 | tf_op jit(solution)/shard_map/ppermute | solution.py:17
  51.2 13.1 %collective-permute-start.3 = (bf16[1,256,1,130]{1,3,2,0:T(8,128)(2,1)S(1)}, bf16[1,256,1,130]{1,3,2,0:T(8,128)(2,1)S(1)}, u32[]{:S(2)}, u32[]{:S(2)}) collective-permute-start(bf16[1,256,1,130]{1,3,2,0:T(8,128)(2,1)S(1)} %get-tuple-element.342), channel_id=1, source_target_pairs={{4,0},{8,4},{12,8},{16,12},{20,16},{24,20},{28,24},{0,28},{5,1},{9... | collective-permute-start | bytes 199688 | tf_op jit(solution)/shard_map/ppermute | solution.py:17
  56.5 17.0 %collective-permute-start.9 = (f32[1,256,1,130]{1,3,2,0:T(8,128)S(1)}, f32[1,256,1,130]{1,3,2,0:T(8,128)S(1)}, u32[]{:S(2)}, u32[]{:S(2)}) collective-permute-start(f32[1,256,1,130]{1,3,2,0:T(8,128)S(1)} %get-tuple-element.326), channel_id=1, source_target_pairs={{4,0},{8,4},{12,8},{16,12},{20,16},{24,20},{28,24},{5,1},{9,5},{13... | collective-permute-start | bytes 399368 | tf_op jit(solution)/shard_map/ppermute | solution.py:17
  57.8 14.8 %collective-permute-start.8 = (f32[1,256,1,130]{1,3,2,0:T(8,128)S(1)}, f32[1,256,1,130]{1,3,2,0:T(8,128)S(1)}, u32[]{:S(2)}, u32[]{:S(2)}) collective-permute-start(f32[1,256,1,130]{1,3,2,0:T(8,128)S(1)} %get-tuple-element.327), channel_id=1, source_target_pairs={{0,4},{4,8},{8,12},{12,16},{16,20},{20,24},{24,28},{1,5},{5,9},{9,... | collective-permute-start | bytes 399368 | tf_op jit(solution)/shard_map/ppermute | solution.py:15
  64.3 6.8 %collective-permute-start.2 = (bf16[1,256,1,130]{1,3,2,0:T(8,128)(2,1)S(1)}, bf16[1,256,1,130]{1,3,2,0:T(8,128)(2,1)S(1)}, u32[]{:S(2)}, u32[]{:S(2)}) collective-permute-start(bf16[1,256,1,130]{1,3,2,0:T(8,128)(2,1)S(1)} %get-tuple-element.343), channel_id=1, source_target_pairs={{0,4},{4,8},{8,12},{12,16},{16,20},{20,24},{24,28},{28,0},{1,5},{5... | collective-permute-start | bytes 199688 | tf_op jit(solution)/shard_map/ppermute | solution.py:15
  72.2 1.3 copy-start.1
  73.6 12.2 %copy-start.5 = (bf16[9,256,256]{2,1,0:T(8,128)(2,1)S(1)}, bf16[9,256,256]{2,1,0:T(8,128)(2,1)}, u32[]{:S(2)}) copy-start(bf16[9,256,256]{2,1,0:T(8,128)(2,1)} %param.58) | copy-start | bytes 3538948
  73.6 6.1 %collective-permute-start.10 = (f32[1,256,8,1]{1,3,2,0:T(1,128)S(1)}, f32[1,256,8,1]{1,3,2,0:T(1,128)S(1)}, u32[]{:S(2)}, u32[]{:S(2)}) collective-permute-start(f32[1,256,8,1]{1,3,2,0:T(1,128)S(1)} %get-tuple-element.333), channel_id=1, source_target_pairs={{0,32},{32,64},{64,96},{96,128},{128,160},{160,192},{192,224},{224... | collective-permute-start | bytes 24584 | tf_op jit(solution)/shard_map/ppermute | solution.py:15
  76.4 2.1 copy-start.8
  79.7 3.7 collective-permute-start.11
  85.7 4.4 copy-start.9
  96.0 46.7 %collective-permute-start.4 = (bf16[1,256,8,1]{1,3,2,0:T(2,128)(2,1)S(1)}, bf16[1,256,8,1]{1,3,2,0:T(2,128)(2,1)S(1)}, u32[]{:S(2)}, u32[]{:S(2)}) collective-permute-start(bf16[1,256,8,1]{1,3,2,0:T(2,128)(2,1)S(1)} %get-tuple-element.344), channel_id=1, source_target_pairs={{0,32},{32,64},{64,96},{96,128},{128,160},{160,192},{192,224},{224... | collective-permute-start | bytes 12296 | tf_op jit(solution)/shard_map/ppermute | solution.py:15
  96.6 46.1 %collective-permute-start.5 = (bf16[1,256,8,1]{1,3,2,0:T(2,128)(2,1)S(1)}, bf16[1,256,8,1]{1,3,2,0:T(2,128)(2,1)S(1)}, u32[]{:S(2)}, u32[]{:S(2)}) collective-permute-start(bf16[1,256,8,1]{1,3,2,0:T(2,128)(2,1)S(1)} %get-tuple-element.345), channel_id=1, source_target_pairs={{32,0},{64,32},{96,64},{128,96},{160,128},{192,160},{224,192},{0,2... | collective-permute-start | bytes 12296 | tf_op jit(solution)/shard_map/ppermute | solution.py:17
  143.4 11.1 %collective-permute-start.7 = (bf16[1,256,1,130]{1,3,2,0:T(8,128)(2,1)}, bf16[1,256,1,130]{1,3,2,0:T(8,128)(2,1)}, u32[]{:S(2)}, u32[]{:S(2)}) collective-permute-start(bf16[1,256,1,130]{1,3,2,0:T(8,128)(2,1)} %get-tuple-element.338), channel_id=1, source_target_pairs={{4,0},{8,4},{12,8},{16,12},{20,16},{24,20},{28,24},{0,28},{5,1},{9... | collective-permute-start | bytes 199688 | tf_op jit(solution)/shard_map/ppermute | solution.py:17
  145.6 5.9 %copy-start.7 = (bf16[1,256,1,130]{1,3,2,0:T(8,128)(2,1)S(1)}, bf16[1,256,1,130]{1,3,2,0:T(8,128)(2,1)}, u32[]{:S(2)}) copy-start(bf16[1,256,1,130]{1,3,2,0:T(8,128)(2,1)} %get-tuple-element.339) | copy-start | bytes 199684
  151.5 6.9 %collective-permute-start.6 = (bf16[1,256,1,130]{1,3,2,0:T(8,128)(2,1)S(1)}, bf16[1,256,1,130]{1,3,2,0:T(8,128)(2,1)S(1)}, u32[]{:S(2)}, u32[]{:S(2)}) collective-permute-start(bf16[1,256,1,130]{1,3,2,0:T(8,128)(2,1)S(1)} %copy-done.7), channel_id=1, source_target_pairs={{0,4},{4,8},{8,12},{12,16},{16,20},{20,24},{24,28},{28,0},{1,5},{5... | collective-permute-start | bytes 199688 | tf_op jit(solution)/shard_map/ppermute | solution.py:15
  160.8 2.1 copy-start.10
  166.5 4.9 %collective-permute-start.12 = (f32[1,256,1,130]{1,3,2,0:T(8,128)S(1)}, f32[1,256,1,130]{1,3,2,0:T(8,128)S(1)}, u32[]{:S(2)}, u32[]{:S(2)}) collective-permute-start(f32[1,256,1,130]{1,3,2,0:T(8,128)S(1)} %get-tuple-element.323), channel_id=1, source_target_pairs={{0,4},{4,8},{8,12},{12,16},{16,20},{20,24},{24,28},{1,5},{5,9},{9,... | collective-permute-start | bytes 399368 | tf_op jit(solution)/shard_map/ppermute | solution.py:15
  169.8 10.4 %copy-start.6 = (bf16[9,256,256]{2,1,0:T(8,128)(2,1)S(1)}, bf16[9,256,256]{2,1,0:T(8,128)(2,1)}, u32[]{:S(2)}) copy-start(bf16[9,256,256]{2,1,0:T(8,128)(2,1)} %param.59) | copy-start | bytes 3538948
  169.9 7.4 %collective-permute-start.13 = (f32[1,256,1,130]{1,3,2,0:T(8,128)S(1)}, f32[1,256,1,130]{1,3,2,0:T(8,128)S(1)}, u32[]{:S(2)}, u32[]{:S(2)}) collective-permute-start(f32[1,256,1,130]{1,3,2,0:T(8,128)S(1)} %get-tuple-element.322), channel_id=1, source_target_pairs={{4,0},{8,4},{12,8},{16,12},{20,16},{24,20},{28,24},{5,1},{9,5},{13... | collective-permute-start | bytes 399368 | tf_op jit(solution)/shard_map/ppermute | solution.py:17
  177.4 1.0 copy-start.2
  178.4 6.9 %collective-permute-start.14 = (f32[1,256,8,1]{1,3,2,0:T(1,128)S(1)}, f32[1,256,8,1]{1,3,2,0:T(1,128)S(1)}, u32[]{:S(2)}, u32[]{:S(2)}) collective-permute-start(f32[1,256,8,1]{1,3,2,0:T(1,128)S(1)} %get-tuple-element.331), channel_id=1, source_target_pairs={{0,32},{32,64},{64,96},{96,128},{128,160},{160,192},{192,224},{224... | collective-permute-start | bytes 24584 | tf_op jit(solution)/shard_map/ppermute | solution.py:15
  180.2 4.9 %copy-start.3 = (f32[1,256,8,130]{1,3,2,0:T(8,128)S(1)}, f32[1,256,8,130]{1,3,2,0:T(8,128)}, u32[]{:S(2)}) copy-start(f32[1,256,8,130]{1,3,2,0:T(8,128)} %copy-done.2) | copy-start | bytes 3194884
  185.2 3.8 collective-permute-start.15
  441.6 3.2 copy-start.4
Sparse Core Ops, SparseCore 0:
  165.9 275.6 all-reduce.4
where the time goes:
time: 455 us; the launch traced here: 454 us
  waiting for transfers between devices  272 us (60%)
  local copies, waits for them, and re-layouts  84.1 us (18%)
  matrix products  46.6 us (10%)
  starting transfers between devices  28.6 us (6%)
  between operations  16.1 us (4%)
  other arithmetic  6.15 us (1%)
    psum x1, waiting for transfers between devices, per_device(): grad_one, grad_two = lax.psum((local_one, local_two), ('lon', 'lat', 'dp'))  251 us
    scatter-add x14, local copies, waits for them, and re-layouts, transposed(): padded_grad = padded_grad.at[:, :, tap_row:tap_row + tile_rows, tap_col:t...  57 us
    dot_general x18, matrix products, transposed(): jnp.einsum('oc,bohw->bchw', weight[3 * tap_row + tap_col], grad_tile, pre...  32.6 us
    ppermute x8, starting transfers between devices, with_halo(): lax.ppermute(tail, axis, [(i, (i + 1) % count) for i in range(ends)])  19.6 us
    unnamed x40, local copies, waits for them, and re-layouts  16.1 us
    ppermute x8, waiting for transfers between devices, with_halo(): lax.ppermute(head, axis, [((i + 1) % count, i) for i in range(ends)])  11.8 us
  transfers between devices with their start and end apart: 17, of which 6 were waited for; matrix products, arithmetic and copies ran while one was open for 23% of the time, Pallas kernels for 0%

commit v1 on v0

--- a/solution.py
+++ b/solution.py
@@ -2,6 +2,7 @@
 import jax.numpy as jnp
 from jax import lax
 from jax.sharding import PartitionSpec as P
+from jax.lax import psum
 
 
 def with_halo(cells, sides, width, closed):
@@ -116,7 +117,8 @@
     local_one = jnp.einsum(
         "bohw,btchw->toc", back_hidden, patch_in, preferred_element_type=jnp.float32
     )
-    grad_one, grad_two = lax.psum((local_one, local_two), ("lon", "lat", "dp"))
+    resolve_ratios = lambda my_tile: psum(psum(my_tile, axis_name="lon"), ("lat", "dp"))
+    grad_one, grad_two = resolve_ratios((local_one, local_two))
     back_fields = returned(transposed(back_hidden, weight_one, tile_rows, tile_cols), edge_info)
     grad_fields = (cotangent.astype(jnp.float32) + back_fields).astype(jnp.bfloat16)
     return (output, grad_fields, grad_one, grad_two)

time: 455 us -> 375 us (0.82)
  waiting for transfers between devices: 272 us -> 186 us
    psum x1 -> x2, waiting for transfers between devices: 251 us -> 162 us  [the longest x1 99.3 us: per_device(): psum(psum(my_tile, axis_name='lon'), ('lat', 'dp'))]
    unnamed x40 -> x46, local copies, waits for them, and re-layouts: 16.1 us -> 16.6 us
  transfers between devices with their start and end apart: 17 -> 18, of which waited for: 6 -> 10; matrix products, arithmetic and copies ran while one was open for 23% -> 30% of each run, Pallas kernels for 0% -> 0%
where the time goes in v1:
time: 375 us; the launch traced here: 371 us
  waiting for transfers between devices  186 us (50%)
  local copies, waits for them, and re-layouts  85.5 us (23%)
  matrix products  47.3 us (13%)
  starting transfers between devices  30.3 us (8%)
  between operations  16.1 us (4%)
  other arithmetic  6.47 us (2%)
    psum x1, waiting for transfers between devices, per_device(): psum(psum(my_tile, axis_name='lon'), ('lat', 'dp'))  99.3 us
    psum x1, waiting for transfers between devices, per_device(): psum(my_tile, axis_name='lon')  62.5 us
    scatter-add x14, local copies, waits for them, and re-layouts, transposed(): padded_grad = padded_grad.at[:, :, tap_row:tap_row + tile_rows, tap_col:t...  56.7 us
    dot_general x18, matrix products, transposed(): jnp.einsum('oc,bohw->bchw', weight[3 * tap_row + tap_col], grad_tile, pre...  33.3 us
    ppermute x8, starting transfers between devices, with_halo(): lax.ppermute(tail, axis, [(i, (i + 1) % count) for i in range(ends)])  20 us
    unnamed x46, local copies, waits for them, and re-layouts  16.6 us
    ppermute x8, waiting for transfers between devices, with_halo(): lax.ppermute(head, axis, [((i + 1) % count, i) for i in range(ends)])  12.3 us
    ppermute x8, waiting for transfers between devices, with_halo(): lax.ppermute(tail, axis, [(i, (i + 1) % count) for i in range(ends)])  11.5 us
  transfers between devices with their start and end apart: 18, of which 10 were waited for; matrix products, arithmetic and copies ran while one was open for 30% of the time, Pallas kernels for 0%

profile of v1, /device:TPU:97, one launch (start us, length us, event | category | flops | bytes accessed | tf_op | source)
XLA Modules:
  0.0 371.2 jit_solution(3184082240792568851)
XLA Ops:
  8.6 2.9 collective-permute-start
  18.0 3.9 %scatter-add.89 = f32[1,256,10,130]{1,3,2,0:T(8,128)S(1)} dynamic-update-slice(f32[1,256,10,130]{1,3,2,0:T(8,128)S(1)} %scatter-add.86, f32[1,256,8,128]{1,3,2,0:T(8,128)S(1)} %fusion.20, s32[]{:T(128)} %constant.657.clone.1, s32[]{:T(128)} %constant.657.clone.1, s32[]{:T(128)} %bitcast.51, s32[]{:T(128)} %bitcast.52) | dynamic-update-slice | bytes 2097156 | tf_op jit(solution)/shard_map/scatter-add | solution.py:82
  21.9 3.2 add_select_fusion.1
  25.1 4.0 %scatter-add.90 = f32[1,256,10,130]{1,3,2,0:T(8,128)S(1)} dynamic-update-slice(f32[1,256,10,130]{1,3,2,0:T(8,128)S(1)} %scatter-add.89, f32[1,256,8,128]{1,3,2,0:T(8,128)S(1)} %add_select_fusion.1, s32[]{:T(128)} %constant.657.clone.1, s32[]{:T(128)} %constant.657.clone.1, s32[]{:T(128)} %bitcast.57, s32[]{:T(128)} %bitcast.58) | dynamic-update-slice | bytes 2097156 | tf_op jit(solution)/shard_map/scatter-add | solution.py:82
  31.6 2.7 scatter-add.94
  35.6 2.7 scatter-add.95
  40.9 2.7 scatter-add.99
  44.9 2.7 scatter-add.100
  50.9 5.2 %collective-permute-start.3 = (bf16[1,256,1,130]{1,3,2,0:T(8,128)(2,1)S(1)}, bf16[1,256,1,130]{1,3,2,0:T(8,128)(2,1)S(1)}, u32[]{:S(2)}, u32[]{:S(2)}) collective-permute-start(bf16[1,256,1,130]{1,3,2,0:T(8,128)(2,1)S(1)} %get-tuple-element.344), channel_id=1, source_target_pairs={{4,0},{8,4},{12,8},{16,12},{20,16},{24,20},{28,24},{0,28},{5,1},{9... | collective-permute-start | bytes 199688 | tf_op jit(solution)/shard_map/ppermute | solution.py:18
  57.5 5.5 %collective-permute-start.8 = (f32[1,256,1,130]{1,3,2,0:T(8,128)S(1)}, f32[1,256,1,130]{1,3,2,0:T(8,128)S(1)}, u32[]{:S(2)}, u32[]{:S(2)}) collective-permute-start(f32[1,256,1,130]{1,3,2,0:T(8,128)S(1)} %get-tuple-element.329), channel_id=1, source_target_pairs={{0,4},{4,8},{8,12},{12,16},{16,20},{20,24},{24,28},{1,5},{5,9},{9,... | collective-permute-start | bytes 399368 | tf_op jit(solution)/shard_map/ppermute | solution.py:16
  64.4 6.4 %collective-permute-done.2 = bf16[1,256,1,130]{1,3,2,0:T(8,128)(2,1)S(1)} collective-permute-done((bf16[1,256,1,130]{1,3,2,0:T(8,128)(2,1)S(1)}, bf16[1,256,1,130]{1,3,2,0:T(8,128)(2,1)S(1)}, u32[]{:S(2)}, u32[]{:S(2)}) %collective-permute-start.2) | collective-permute-done | bytes 66592 | tf_op jit(solution)/shard_map/ppermute | solution.py:16
  73.3 2.7 collective-permute-start.10
  85.5 4.4 %multiply_convert_fusion = (bf16[1,256,8,128]{1,3,2,0:T(8,128)(2,1)S(1)}, bf16[1,256,8,128]{1,3,2,0:T(8,128)(2,1)S(1)}) fusion(f32[1,256,8,128]{1,3,2,0:T(8,128)} %scatter-add.106, bf16[9,256,256]{2,1,0:T(8,128)(2,1)S(1)} %copy-done.5, bf16[1,9,256,8,128]{2,4,1,3,0:T(8,128)(2,1)} %copy-done.11), kind=kOutput, calls=%fused_computation.55 | convolution fusion | flops 1210843136 | bytes 7995392 | tf_op jit(solution)/shard_map/toc,btchw->bohw/dot_general | solution.py:66
  94.9 2.9 fusion.8
  97.8 3.0 collective-permute-start.6
  101.1 3.7 collective-permute-done.6
  111.6 2.9 fusion.11
  114.9 3.3 fusion.29
  118.3 7.1 %scatter-add.110 = f32[1,256,10,130]{1,3,2,0:T(8,128)S(1)} dynamic-update-slice(f32[1,256,10,130]{1,3,2,0:T(8,128)S(1)} %scatter-add.109, f32[1,256,8,128]{1,3,2,0:T(8,128)} %fusion.29, s32[]{:T(128)} %constant.657.clone.1, s32[]{:T(128)} %constant.657.clone.1, s32[]{:T(128)} %bitcast.51, s32[]{:T(128)} %bitcast.52) | dynamic-update-slice | bytes 2097156 | tf_op jit(solution)/shard_map/scatter-add | solution.py:82
  125.4 4.1 %add_select_fusion = f32[1,256,8,128]{1,3,2,0:T(8,128)} fusion(f32[1,256,10,130]{1,3,2,0:T(8,128)S(1)} %scatter-add.110, s32[]{:T(128)} %bitcast.57, s32[]{:T(128)} %bitcast.58, bf16[1,256,8,128]{1,3,2,0:T(8,128)(2,1)S(1)} %get-tuple-element.336, pred[]{:T(512)} %and_reduce_fusion, bf16[9,256,256]{2,1,0:T(8,128)(2,1)} %param.58), kind=kOutput, calls=%fused_computation.10 | convolution fusion | flops 134742016 | bytes 2754048 | tf_op jit(solution)/shard_map/oc,bohw->bchw/dot_general | solution.py:74
  129.5 7.2 %scatter-add.111 = f32[1,256,10,130]{1,3,2,0:T(8,128)S(1)} dynamic-update-slice(f32[1,256,10,130]{1,3,2,0:T(8,128)S(1)} %scatter-add.110, f32[1,256,8,128]{1,3,2,0:T(8,128)} %add_select_fusion, s32[]{:T(128)} %constant.657.clone.1, s32[]{:T(128)} %constant.657.clone.1, s32[]{:T(128)} %bitcast.57, s32[]{:T(128)} %bitcast.58) | dynamic-update-slice | bytes 2097156 | tf_op jit(solution)/shard_map/scatter-add | solution.py:82
  140.1 5.9 %scatter-add.115 = f32[1,256,10,130]{1,3,2,0:T(8,128)S(1)} dynamic-update-slice(f32[1,256,10,130]{1,3,2,0:T(8,128)S(1)} %fusion.31, f32[1,256,8,128]{1,3,2,0:T(8,128)} %fusion.32, s32[]{:T(128)} %constant.657.clone.1, s32[]{:T(128)} %constant.657.clone.1, s32[]{:T(128)} %constant.670.clone.1, s32[]{:T(128)} %constant.670.clone.1) | dynamic-update-slice | bytes 2097156 | tf_op jit(solution)/shard_map/scatter-add | solution.py:82
  148.1 5.9 %scatter-add.116 = f32[1,256,10,130]{1,3,2,0:T(8,128)S(1)} dynamic-update-slice(f32[1,256,10,130]{1,3,2,0:T(8,128)S(1)} %scatter-add.115, f32[1,256,8,128]{1,3,2,0:T(8,128)} %fusion.33, s32[]{:T(128)} %constant.657.clone.1, s32[]{:T(128)} %constant.657.clone.1, s32[]{:T(128)} %constant.670.clone.1, s32[]{:T(128)} %constant.667.clone.1) | dynamic-update-slice | bytes 2097156 | tf_op jit(solution)/shard_map/scatter-add | solution.py:82
  157.4 5.9 %scatter-add.120 = f32[1,256,10,130]{1,3,2,0:T(8,128)S(1)} dynamic-update-slice(f32[1,256,10,130]{1,3,2,0:T(8,128)S(1)} %fusion.35, f32[1,256,8,128]{1,3,2,0:T(8,128)} %fusion.36, s32[]{:T(128)} %constant.657.clone.1, s32[]{:T(128)} %constant.657.clone.1, s32[]{:T(128)} %constant.667.clone.1, s32[]{:T(128)} %constant.670.clone.1) | dynamic-update-slice | bytes 2097156 | tf_op jit(solution)/shard_map/scatter-add | solution.py:82
  165.5 5.9 %scatter-add.121 = f32[1,256,10,130]{1,3,2,0:T(8,128)S(1)} dynamic-update-slice(f32[1,256,10,130]{1,3,2,0:T(8,128)S(1)} %scatter-add.120, f32[1,256,8,128]{1,3,2,0:T(8,128)} %fusion.37, s32[]{:T(128)} %constant.657.clone.1, s32[]{:T(128)} %constant.657.clone.1, s32[]{:T(128)} %constant.667.clone.1, s32[]{:T(128)} %constant.667.clone.1) | dynamic-update-slice | bytes 2097156 | tf_op jit(solution)/shard_map/scatter-add | solution.py:82
  171.3 62.5 %all-reduce.9.cloned.1.call-done = (f32[9,256,256]{1,2,0:T(8,128)}, f32[9,256,256]{1,2,0:T(8,128)}) async-done(((f32[9,256,256]{1,2,0:T(8,128)}, f32[9,256,256]{1,2,0:T(8,128)}), (f32[9,256,256]{1,2,0:T(8,128)}, f32[9,256,256]{1,2,0:T(8,128)})) %all-reduce.9.cloned.1.call-update) | async-done | bytes 4718608 | tf_op jit(solution)/shard_map/psum | solution.py:120
  235.2 4.9 %collective-permute-start.12 = (f32[1,256,1,130]{1,3,2,0:T(8,128)}, f32[1,256,1,130]{1,3,2,0:T(8,128)S(1)}, u32[]{:S(2)}, u32[]{:S(2)}) collective-permute-start(f32[1,256,1,130]{1,3,2,0:T(8,128)} %get-tuple-element.325), channel_id=1, source_target_pairs={{0,4},{4,8},{8,12},{12,16},{16,20},{20,24},{24,28},{1,5},{5,9},{9,... | collective-permute-start | bytes 399368 | tf_op jit(solution)/shard_map/ppermute | solution.py:16
  242.3 5.6 %collective-permute-done.13 = f32[1,256,1,130]{1,3,2,0:T(8,128)S(1)} collective-permute-done((f32[1,256,1,130]{1,3,2,0:T(8,128)S(1)}, f32[1,256,1,130]{1,3,2,0:T(8,128)S(1)}, u32[]{:S(2)}, u32[]{:S(2)}) %collective-permute-start.13) | collective-permute-done | bytes 133152 | tf_op jit(solution)/shard_map/ppermute | solution.py:18
  249.4 3.8 %fusion.41 = bf16[1,256,8,128]{1,3,2,0:T(8,128)(2,1)S(1)} fusion(bf16[1,9,256,8,128]{2,4,3,1,0:T(8,128)(2,1)} %copy-done.13, bf16[9,256,256]{2,1,0:T(8,128)(2,1)S(1)} %copy-done.6, bf16[1,256,8,128]{1,3,2,0:T(8,128)(2,1)S(1)} %copy.9), kind=kOutput, calls=%fused_computation.51 | convolution fusion | flops 1208745984 | bytes 6946816 | tf_op jit(solution)/shard_map/toc,btchw->bohw/dot_general | solution.py:66
  255.8 2.8 collective-permute-done.15
  259.9 99.3 %all-reduce.7.cloned.1.call-done = (f32[9,256,256]{1,2,0:T(8,128)}, f32[9,256,256]{1,2,0:T(8,128)}) async-done(((f32[9,256,256]{1,2,0:T(8,128)}, f32[9,256,256]{1,2,0:T(8,128)}), (f32[9,256,256]{1,2,0:T(8,128)}, f32[9,256,256]{1,2,0:T(8,128)})) %all-reduce.7.cloned.1.call-update) | async-done | bytes 4718608 | tf_op jit(solution)/shard_map/psum | solution.py:120
  359.2 3.2 copy.38
  (145 shorter events, 66.4 us)
Async XLA Ops:
  7.2 7.0 %copy-start = (bf16[1,256,8,128]{3,2,1,0:T(8,128)(2,1)S(1)}, bf16[1,256,8,128]{3,2,1,0:T(8,128)(2,1)}, u32[]{:S(2)}) copy-start(bf16[1,256,8,128]{3,2,1,0:T(8,128)(2,1)} %param.61) | copy-start | bytes 1572868
  7.2 226.6 %all-reduce.9.cloned.1.call-start = ((), (), s32[]{:S(2)}) async-start(), calls=%async_computation.1 | async-start | bytes 9437184 | tf_op jit(solution)/shard_map/psum | solution.py:120
  8.6 42.3 %collective-permute-start = (bf16[1,256,8,1]{1,3,2,0:T(2,128)(2,1)S(1)}, bf16[1,256,8,1]{1,3,2,0:T(2,128)(2,1)S(1)}, u32[]{:S(2)}, u32[]{:S(2)}) collective-permute-start(bf16[1,256,8,1]{1,3,2,0:T(2,128)(2,1)S(1)} %get-tuple-element.348), channel_id=1, source_target_pairs={{0,32},{32,64},{64,96},{96,128},{128,160},{160,192},{192,224},{224... | collective-permute-start | bytes 12296 | tf_op jit(solution)/shard_map/ppermute | solution.py:16
  11.5 39.3 %collective-permute-start.1 = (bf16[1,256,8,1]{1,3,2,0:T(2,128)(2,1)S(1)}, bf16[1,256,8,1]{1,3,2,0:T(2,128)(2,1)S(1)}, u32[]{:S(2)}, u32[]{:S(2)}) collective-permute-start(bf16[1,256,8,1]{1,3,2,0:T(2,128)(2,1)S(1)} %get-tuple-element.349), channel_id=1, source_target_pairs={{32,0},{64,32},{96,64},{128,96},{160,128},{192,160},{224,192},{0,2... | collective-permute-start | bytes 12296 | tf_op jit(solution)/shard_map/ppermute | solution.py:18
  50.9 13.1 %collective-permute-start.3 = (bf16[1,256,1,130]{1,3,2,0:T(8,128)(2,1)S(1)}, bf16[1,256,1,130]{1,3,2,0:T(8,128)(2,1)S(1)}, u32[]{:S(2)}, u32[]{:S(2)}) collective-permute-start(bf16[1,256,1,130]{1,3,2,0:T(8,128)(2,1)S(1)} %get-tuple-element.344), channel_id=1, source_target_pairs={{4,0},{8,4},{12,8},{16,12},{20,16},{24,20},{28,24},{0,28},{5,1},{9... | collective-permute-start | bytes 199688 | tf_op jit(solution)/shard_map/ppermute | solution.py:18
  56.2 17.0 %collective-permute-start.9 = (f32[1,256,1,130]{1,3,2,0:T(8,128)S(1)}, f32[1,256,1,130]{1,3,2,0:T(8,128)S(1)}, u32[]{:S(2)}, u32[]{:S(2)}) collective-permute-start(f32[1,256,1,130]{1,3,2,0:T(8,128)S(1)} %get-tuple-element.328), channel_id=1, source_target_pairs={{4,0},{8,4},{12,8},{16,12},{20,16},{24,20},{28,24},{5,1},{9,5},{13... | collective-permute-start | bytes 399368 | tf_op jit(solution)/shard_map/ppermute | solution.py:18
  57.5 14.8 %collective-permute-start.8 = (f32[1,256,1,130]{1,3,2,0:T(8,128)S(1)}, f32[1,256,1,130]{1,3,2,0:T(8,128)S(1)}, u32[]{:S(2)}, u32[]{:S(2)}) collective-permute-start(f32[1,256,1,130]{1,3,2,0:T(8,128)S(1)} %get-tuple-element.329), channel_id=1, source_target_pairs={{0,4},{4,8},{8,12},{12,16},{16,20},{20,24},{24,28},{1,5},{5,9},{9,... | collective-permute-start | bytes 399368 | tf_op jit(solution)/shard_map/ppermute | solution.py:16
  64.1 6.8 %collective-permute-start.2 = (bf16[1,256,1,130]{1,3,2,0:T(8,128)(2,1)S(1)}, bf16[1,256,1,130]{1,3,2,0:T(8,128)(2,1)S(1)}, u32[]{:S(2)}, u32[]{:S(2)}) collective-permute-start(bf16[1,256,1,130]{1,3,2,0:T(8,128)(2,1)S(1)} %get-tuple-element.345), channel_id=1, source_target_pairs={{0,4},{4,8},{8,12},{12,16},{16,20},{20,24},{24,28},{28,0},{1,5},{5... | collective-permute-start | bytes 199688 | tf_op jit(solution)/shard_map/ppermute | solution.py:16
  71.9 1.3 copy-start.1
  73.3 12.2 %copy-start.5 = (bf16[9,256,256]{2,1,0:T(8,128)(2,1)S(1)}, bf16[9,256,256]{2,1,0:T(8,128)(2,1)}, u32[]{:S(2)}) copy-start(bf16[9,256,256]{2,1,0:T(8,128)(2,1)} %param.58) | copy-start | bytes 3538948
  73.3 6.1 %collective-permute-start.10 = (f32[1,256,8,1]{1,3,2,0:T(1,128)S(1)}, f32[1,256,8,1]{1,3,2,0:T(1,128)S(1)}, u32[]{:S(2)}, u32[]{:S(2)}) collective-permute-start(f32[1,256,8,1]{1,3,2,0:T(1,128)S(1)} %get-tuple-element.335), channel_id=1, source_target_pairs={{0,32},{32,64},{64,96},{96,128},{128,160},{160,192},{192,224},{224... | collective-permute-start | bytes 24584 | tf_op jit(solution)/shard_map/ppermute | solution.py:16
  76.2 2.2 copy-start.11
  79.4 3.7 %collective-permute-start.11 = (f32[1,256,8,1]{1,3,2,0:T(1,128)S(1)}, f32[1,256,8,1]{1,3,2,0:T(1,128)S(1)}, u32[]{:S(2)}, u32[]{:S(2)}) collective-permute-start(f32[1,256,8,1]{1,3,2,0:T(1,128)S(1)} %get-tuple-element.334), channel_id=1, source_target_pairs={{32,0},{64,32},{96,64},{128,96},{160,128},{192,160},{224,192},{0,2... | collective-permute-start | bytes 24584 | tf_op jit(solution)/shard_map/ppermute | solution.py:18
  85.5 9.4 %copy-start.12 = (bf16[1,9,256,8,128]{2,4,1,3,0:T(8,128)(2,1)S(1)}, bf16[1,9,256,8,128]{2,4,1,3,0:T(8,128)(2,1)}, u32[]{:S(2)}) copy-start(bf16[1,9,256,8,128]{2,4,1,3,0:T(8,128)(2,1)} %copy-done.11) | copy-start | bytes 14155780
  89.9 2.6 collective-permute-start.4
  90.5 3.7 %collective-permute-start.5 = (bf16[1,256,8,1]{1,3,2,0:T(2,128)(2,1)S(1)}, bf16[1,256,8,1]{1,3,2,0:T(2,128)(2,1)S(1)}, u32[]{:S(2)}, u32[]{:S(2)}) collective-permute-start(bf16[1,256,8,1]{1,3,2,0:T(2,128)(2,1)S(1)} %get-tuple-element.347), channel_id=1, source_target_pairs={{32,0},{64,32},{96,64},{128,96},{160,128},{192,160},{224,192},{0,2... | collective-permute-start | bytes 12296 | tf_op jit(solution)/shard_map/ppermute | solution.py:18
  92.5 2.4 copy-start.9
  94.2 0.7 copy-start.7
  94.9 5.9 %collective-permute-start.7 = (bf16[1,256,1,130]{1,3,2,0:T(8,128)(2,1)S(1)}, bf16[1,256,1,130]{1,3,2,0:T(8,128)(2,1)S(1)}, u32[]{:S(2)}, u32[]{:S(2)}) collective-permute-start(bf16[1,256,1,130]{1,3,2,0:T(8,128)(2,1)S(1)} %get-tuple-element.340), channel_id=1, source_target_pairs={{4,0},{8,4},{12,8},{16,12},{20,16},{24,20},{28,24},{0,28},{5,1},{9... | collective-permute-start | bytes 199688 | tf_op jit(solution)/shard_map/ppermute | solution.py:18
  97.8 7.0 %collective-permute-start.6 = (bf16[1,256,1,130]{1,3,2,0:T(8,128)(2,1)}, bf16[1,256,1,130]{1,3,2,0:T(8,128)(2,1)S(1)}, u32[]{:S(2)}, u32[]{:S(2)}) collective-permute-start(bf16[1,256,1,130]{1,3,2,0:T(8,128)(2,1)} %get-tuple-element.341), channel_id=1, source_target_pairs={{0,4},{4,8},{8,12},{12,16},{16,20},{20,24},{24,28},{28,0},{1,5},{5... | collective-permute-start | bytes 199688 | tf_op jit(solution)/shard_map/ppermute | solution.py:16
  108.1 0.7 copy-start.10
  108.3 0.7 copy-start.8
  109.4 2.2 copy-start.13
  114.5 244.7 %all-reduce.7.cloned.1.call-start = ((), (), s32[]{:S(2)}) async-start(), calls=%async_computation | async-start | bytes 9437184 | tf_op jit(solution)/shard_map/psum | solution.py:120
  235.2 7.1 %collective-permute-start.12 = (f32[1,256,1,130]{1,3,2,0:T(8,128)}, f32[1,256,1,130]{1,3,2,0:T(8,128)S(1)}, u32[]{:S(2)}, u32[]{:S(2)}) collective-permute-start(f32[1,256,1,130]{1,3,2,0:T(8,128)} %get-tuple-element.325), channel_id=1, source_target_pairs={{0,4},{4,8},{8,12},{12,16},{16,20},{20,24},{24,28},{1,5},{5,9},{9,... | collective-permute-start | bytes 399368 | tf_op jit(solution)/shard_map/ppermute | solution.py:16
  240.3 9.0 %copy-start.6 = (bf16[9,256,256]{2,1,0:T(8,128)(2,1)S(1)}, bf16[9,256,256]{2,1,0:T(8,128)(2,1)}, u32[]{:S(2)}) copy-start(bf16[9,256,256]{2,1,0:T(8,128)(2,1)} %param.59) | copy-start | bytes 3538948
  240.4 7.4 %collective-permute-start.13 = (f32[1,256,1,130]{1,3,2,0:T(8,128)S(1)}, f32[1,256,1,130]{1,3,2,0:T(8,128)S(1)}, u32[]{:S(2)}, u32[]{:S(2)}) collective-permute-start(f32[1,256,1,130]{1,3,2,0:T(8,128)S(1)} %get-tuple-element.324), channel_id=1, source_target_pairs={{4,0},{8,4},{12,8},{16,12},{20,16},{24,20},{28,24},{5,1},{9,5},{13... | collective-permute-start | bytes 399368 | tf_op jit(solution)/shard_map/ppermute | solution.py:18
  247.9 1.0 copy-start.2
  248.9 6.8 %collective-permute-start.14 = (f32[1,256,8,1]{1,3,2,0:T(1,128)S(1)}, f32[1,256,8,1]{1,3,2,0:T(1,128)S(1)}, u32[]{:S(2)}, u32[]{:S(2)}) collective-permute-start(f32[1,256,8,1]{1,3,2,0:T(1,128)S(1)} %get-tuple-element.333), channel_id=1, source_target_pairs={{0,32},{32,64},{64,96},{96,128},{128,160},{160,192},{192,224},{224... | collective-permute-start | bytes 24584 | tf_op jit(solution)/shard_map/ppermute | solution.py:16
  249.4 4.9 %copy-start.3 = (f32[1,256,8,130]{1,3,2,0:T(8,128)S(1)}, f32[1,256,8,130]{1,3,2,0:T(8,128)}, u32[]{:S(2)}) copy-start(f32[1,256,8,130]{1,3,2,0:T(8,128)} %copy-done.2) | copy-start | bytes 3194884
  254.4 4.2 %collective-permute-start.15 = (f32[1,256,8,1]{1,3,2,0:T(1,128)S(1)}, f32[1,256,8,1]{1,3,2,0:T(1,128)S(1)}, u32[]{:S(2)}, u32[]{:S(2)}) collective-permute-start(f32[1,256,8,1]{1,3,2,0:T(1,128)S(1)} %get-tuple-element.332), channel_id=1, source_target_pairs={{32,0},{64,32},{96,64},{128,96},{160,128},{192,160},{224,192},{0,2... | collective-permute-start | bytes 24584 | tf_op jit(solution)/shard_map/ppermute | solution.py:18
  359.2 3.2 copy-start.4
Sparse Core Ops, SparseCore 0:
  114.6 119.1 all-reduce.8
  237.2 121.9 all-reduce.6
